TPU v7x, 512 devices: a whole 4x4x16 slice. The times are simulated.
512 devices in a mesh: lag: 64 (over z, y), par: 8 (over x, core).
Axes of the slice: x: 4, y: 4, z: 16, core: 2. Of those that a mesh axis runs over, the one named last changes fastest.
Arguments:
- prior_rows: bfloat16 [64, 512, 16384], P('lag', None, 'par'), may hold values from -0.0625 to 0.0625
- raw_rows: bfloat16 [64, 512, 16384], P('lag', None, 'par'), may hold values from -6 to 6
Outputs:
- diag_zero: float32 [64, 512, 512], P('lag', 'par')
- diag_one: float32 [64, 512, 512], P('lag', 'par')
All inputs are finite; a program needn't handle non-finite values.
Results may differ from a plain program's by a relative error of at most 0.0003.
Values may be sent and summed in bfloat16 or wider, within the bound.
No kernel may reach another device: no remote copies, remote signals or barrier semaphores. Data moves between devices by JAX's collectives and lax.ppermute only.
A program may use at most 64 MiB of HBM per device.

v0:
```python
import jax
import jax.numpy as jnp
from jax import lax
from jax.sharding import PartitionSpec as P


def passed_along(block, axis, distance):
    devices = range(lax.axis_size(axis))
    route = [(i - distance, i) for i in devices if i - distance in devices]
    return lax.ppermute(block, axis, route)


def carried_in(part, axis, combine, identity):
    place = lax.axis_index(axis)
    gathered = lax.all_gather(part, axis)
    state = jnp.zeros_like(part) + jnp.asarray(identity, part.dtype)

    def one(turn, state):
        return combine(state, lax.dynamic_index_in_dim(gathered, turn, 0, False))

    return lax.fori_loop(0, place, one, state)


def add_terms(earlier_term, later_term):
    return earlier_term + later_term


def body(prior_rows, raw_rows):
    incoming = passed_along(raw_rows, "lag", -1)
    following = jnp.concatenate([raw_rows[1:], incoming], axis=0)
    offset_zero = jnp.einsum(
        "lsp,ltp->lst", prior_rows, raw_rows, preferred_element_type=jnp.float32
    )
    offset_one = jnp.einsum(
        "lsp,ltp->lst", prior_rows, following, preferred_element_type=jnp.float32
    )
    stacked = jnp.stack([offset_zero, offset_one], axis=0)
    summed = lax.psum(stacked, "par")
    row_count = summed.shape[2] // lax.axis_size("par")
    shares = lax.dynamic_slice_in_dim(summed, lax.axis_index("par") * row_count, row_count, 2)
    running = jnp.cumsum(shares, axis=1)
    totals = running[:, -1]
    earlier = carried_in(totals, "lag", add_terms, jnp.zeros_like(totals))
    result = running + earlier[:, None]
    return (result[0], result[1])


def solution(mesh):
    in_specs = (P("lag", None, "par"), P("lag", None, "par"))
    out_specs = (P("lag", "par", None), P("lag", "par", None))
    return jax.shard_map(body, mesh=mesh, in_specs=in_specs, out_specs=out_specs, check_vma=False)
```

profile of v0, /device:TPU:504, one launch (start us, length us, event | category | flops | bytes accessed | tf_op | source)
XLA Modules:
  0.0 406.9 jit_solution(13441115809973751010)
XLA Ops:
  7.2 2.9 collective-permute-start
  10.2 2.9 fusion.6
  13.0 42.2 %collective-permute-done = bf16[1,512,2048]{2,1,0:T(8,128)(2,1)S(1)} collective-permute-done((bf16[1,512,2048]{2,1,0:T(8,128)(2,1)}, bf16[1,512,2048]{2,1,0:T(8,128)(2,1)S(1)}, u32[]{:S(2)}, u32[]{:S(2)}) %collective-permute-start) | collective-permute-done | bytes 2097184 | tf_op jit(solution)/shard_map/ppermute | solution.py:10
  55.2 1.3 fusion.11
  56.5 1.5 pad_maximum_fusion
  58.1 83.5 %all-reduce.2.cloned.1.call-done = f32[2,1,512,512]{3,2,1,0:T(8,128)} async-done(((f32[2,1,512,512]{3,2,1,0:T(8,128)}), f32[2,1,512,512]{3,2,1,0:T(8,128)}) %all-reduce.2.cloned.1.call-update) | async-done | bytes 2097168 | tf_op jit(solution)/shard_map/psum | solution.py:38
  141.5 1.7 constant_dynamic-slice_fusion
  143.2 189.3 %all-gather.3.cloned.1.call-done = f32[128,1,64,512]{3,2,1,0:T(8,128)} async-done(((f32[2,1,64,512]{3,2,1,0:T(8,128)}), f32[128,1,64,512]{3,2,1,0:T(8,128)}) %all-gather.3.cloned.1.call-update) | async-done | bytes 16777232 | tf_op jit(solution)/shard_map/all_gather | solution.py:15
  332.6 65.8 %while.10 = (s32[]{:T(128)}, f32[2,64,512]{2,1,0:T(8,128)S(1)}, s32[]{:T(128)}, f32[64,2,64,512]{3,2,1,0:T(8,128)}, s32[]{:T(128)}, /*index=5*/s32[]{:T(128)}, s32[]{:T(128)}) while((s32[]{:T(128)}, f32[2,64,512]{2,1,0:T(8,128)S(1)}, s32[]{:T(128)}, f32[64,2,64,512]{3,2,1,0:T(8,128)}, s32[]{:T(128)}, /*index=5*/s32[]{:T(128)}, s32[]{:T(128)}) %tuple.30), condition=%wide.region_2.3_spmd, body=%wide.region_1.0_spmd.sunk | while | flops 65541 | bytes 786555 | solution.py:21
  332.6 1.0 bitcast_add_fusion.3
  333.6 1.0 bitcast_add_fusion.3
  334.7 1.0 bitcast_add_fusion.3
  335.7 1.0 bitcast_add_fusion.3
  336.8 1.0 bitcast_add_fusion.3
  337.8 1.0 bitcast_add_fusion.3
  338.9 1.0 bitcast_add_fusion.3
  339.9 1.0 bitcast_add_fusion.3
  340.9 1.0 bitcast_add_fusion.3
  342.0 1.0 bitcast_add_fusion.3
  343.0 1.0 bitcast_add_fusion.3
  344.1 1.0 bitcast_add_fusion.3
  345.1 1.0 bitcast_add_fusion.3
  346.2 1.0 bitcast_add_fusion.3
  347.2 1.0 bitcast_add_fusion.3
  348.3 1.0 bitcast_add_fusion.3
  349.3 1.0 bitcast_add_fusion.3
  350.3 1.0 bitcast_add_fusion.3
  351.4 1.0 bitcast_add_fusion.3
  352.4 1.0 bitcast_add_fusion.3
  353.5 1.0 bitcast_add_fusion.3
  354.5 1.0 bitcast_add_fusion.3
  355.6 1.0 bitcast_add_fusion.3
  356.6 1.0 bitcast_add_fusion.3
  357.7 1.0 bitcast_add_fusion.3
  358.7 1.0 bitcast_add_fusion.3
  359.7 1.0 bitcast_add_fusion.3
  360.8 1.0 bitcast_add_fusion.3
  361.8 1.0 bitcast_add_fusion.3
  362.9 1.0 bitcast_add_fusion.3
  363.9 1.0 bitcast_add_fusion.3
  365.0 1.0 bitcast_add_fusion.3
  366.0 1.0 bitcast_add_fusion.3
  367.1 1.0 bitcast_add_fusion.3
  368.1 1.0 bitcast_add_fusion.3
  369.1 1.0 bitcast_add_fusion.3
  370.2 1.0 bitcast_add_fusion.3
  371.2 1.0 bitcast_add_fusion.3
  372.3 1.0 bitcast_add_fusion.3
  373.3 1.0 bitcast_add_fusion.3
  374.4 1.0 bitcast_add_fusion.3
  375.4 1.0 bitcast_add_fusion.3
  376.5 1.0 bitcast_add_fusion.3
  377.5 1.0 bitcast_add_fusion.3
  378.5 1.0 bitcast_add_fusion.3
  379.6 1.0 bitcast_add_fusion.3
  380.6 1.0 bitcast_add_fusion.3
  381.7 1.0 bitcast_add_fusion.3
  382.7 1.0 bitcast_add_fusion.3
  383.8 1.0 bitcast_add_fusion.3
  384.8 1.0 bitcast_add_fusion.3
  386.9 1.0 bitcast_add_fusion.3
  389.0 1.0 bitcast_add_fusion.3
  391.1 1.0 bitcast_add_fusion.3
  393.2 1.0 bitcast_add_fusion.3
  (17 shorter events, 10.0 us)
Async XLA Ops:
  7.2 3.0 copy-start
  7.2 134.4 %all-reduce.2.cloned.1.call-start = ((), (), s32[]{:S(2)}) async-start(), calls=%async_computation | async-start | bytes 4194304 | tf_op jit(solution)/shard_map/psum | solution.py:38
  7.2 48.0 %collective-permute-start = (bf16[1,512,2048]{2,1,0:T(8,128)(2,1)}, bf16[1,512,2048]{2,1,0:T(8,128)(2,1)S(1)}, u32[]{:S(2)}, u32[]{:S(2)}) collective-permute-start(bf16[1,512,2048]{2,1,0:T(8,128)(2,1)} %param.5), channel_id=1, source_target_pairs={{8,0},{16,8},{24,16},{32,24},{40,32},{48,40},{56,48},{64,56},{72,6... | collective-permute-start | bytes 6291464 | tf_op jit(solution)/shard_map/ppermute | solution.py:10
  58.0 274.5 %all-gather.3.cloned.1.call-start = ((), (), s32[]{:S(2)}) async-start(), calls=%async_computation.1 | async-start | bytes 17039360 | tf_op jit(solution)/shard_map/all_gather | solution.py:15
Sparse Core Ops, SparseCore 0:
  58.2 83.3 all-reduce.1
  144.5 188.0 all-gather.2
where the time goes:
time: 409 us; the launch traced here: 407 us
  waiting for transfers between devices  315 us (77%)
  other arithmetic  66.9 us (16%)
  between operations  14.1 us (3%)
  matrix products  4.16 us (1%)
    all_gather x1, waiting for transfers between devices, carried_in(): gathered = lax.all_gather(part, axis)  189 us
    psum x1, waiting for transfers between devices, body(): summed = lax.psum(stacked, 'par')  83.5 us
    add x63, other arithmetic, add_terms(): return earlier_term + later_term  64.4 us
    ppermute x1, waiting for transfers between devices, passed_along(): return lax.ppermute(block, axis, route)  42.2 us
  transfers between devices with their start and end apart: 3, of which 3 were waited for; matrix products, arithmetic and copies ran while one was open for 1% of the time, Pallas kernels for 0%

commit v1 on v0

--- a/solution.py
+++ b/solution.py
@@ -35,7 +35,11 @@
         "lsp,ltp->lst", prior_rows, following, preferred_element_type=jnp.float32
     )
     stacked = jnp.stack([offset_zero, offset_one], axis=0)
-    summed = lax.psum(stacked, "par")
+
+    def clear_stacks_all_up(incoming_x, row_axis):
+        return lax.all_gather(incoming_x, row_axis).sum(axis=0)
+
+    summed = clear_stacks_all_up(stacked, "par")
     row_count = summed.shape[2] // lax.axis_size("par")
     shares = lax.dynamic_slice_in_dim(summed, lax.axis_index("par") * row_count, row_count, 2)
     running = jnp.cumsum(shares, axis=1)

time: 409 us -> 430 us (1.051)
  waiting for transfers between devices: 315 us -> 326 us
  other arithmetic: 66.9 us -> 76.3 us
    all_gather x0 -> x1, waiting for transfers between devices: none -> 95 us  [clear_stacks_all_up(): return lax.all_gather(incoming_x, row_axis).sum(axis=0)]
    psum x1 -> x0, waiting for transfers between devices: 83.5 us -> none  [body(): summed = lax.psum(stacked, 'par')]
    reduce_sum x0 -> x1, other arithmetic: none -> 9.43 us  [clear_stacks_all_up(): return lax.all_gather(incoming_x, row_axis).sum(axis=0)]
where the time goes in v1:
time: 430 us; the launch traced here: 428 us
  waiting for transfers between devices  326 us (76%)
  other arithmetic  76.3 us (18%)
  between operations  14.1 us (3%)
    all_gather x1, waiting for transfers between devices, carried_in(): gathered = lax.all_gather(part, axis)  189 us
    all_gather x1, waiting for transfers between devices, clear_stacks_all_up(): return lax.all_gather(incoming_x, row_axis).sum(axis=0)  95 us
    add x63, other arithmetic, add_terms(): return earlier_term + later_term  64.4 us
    ppermute x1, waiting for transfers between devices, passed_along(): return lax.ppermute(block, axis, route)  42.2 us
    reduce_sum x1, other arithmetic, clear_stacks_all_up(): return lax.all_gather(incoming_x, row_axis).sum(axis=0)  9.43 us
  transfers between devices with their start and end apart: 3, of which 3 were waited for; matrix products, arithmetic and copies ran while one was open for 1% of the time, Pallas kernels for 0%

profile of v1, /device:TPU:504, one launch (start us, length us, event | category | flops | bytes accessed | tf_op | source)
XLA Modules:
  0.0 427.7 jit_solution(11075137113260490227)
XLA Ops:
  7.2 2.9 collective-permute-start
  10.2 2.9 fusion.6
  13.0 42.2 %collective-permute-done = bf16[1,512,2048]{2,1,0:T(8,128)(2,1)S(1)} collective-permute-done((bf16[1,512,2048]{2,1,0:T(8,128)(2,1)}, bf16[1,512,2048]{2,1,0:T(8,128)(2,1)S(1)}, u32[]{:S(2)}, u32[]{:S(2)}) %collective-permute-start) | collective-permute-done | bytes 2097184 | tf_op jit(solution)/shard_map/ppermute | solution.py:10
  55.2 1.3 fusion.11
  56.5 1.5 pad_maximum_fusion
  58.1 95.0 %all-gather.5.cloned.1.call-done = f32[16,1,512,512]{3,2,1,0:T(8,128)} async-done(((f32[2,1,512,512]{3,2,1,0:T(8,128)}), f32[16,1,512,512]{3,2,1,0:T(8,128)}) %all-gather.5.cloned.1.call-update) | async-done | bytes 16777232 | tf_op jit(solution)/shard_map/all_gather | solution.py:40
  153.0 9.4 %bitcast_reduce_fusion = f32[2,512,512]{2,1,0:T(8,128)} fusion(f32[8,2,512,512]{3,2,1,0:T(8,128)} %bitcast.31), kind=kLoop, calls=%fused_computation.1 | loop fusion | flops 3670016 | bytes 18874368 | tf_op jit(solution)/shard_map/reduce_sum | solution.py:40
  162.5 1.7 constant_dynamic-slice_fusion
  164.2 189.2 %all-gather.7.cloned.1.call-done = f32[128,64,512]{2,1,0:T(8,128)} async-done(((f32[2,64,512]{2,1,0:T(8,128)}), f32[128,64,512]{2,1,0:T(8,128)}) %all-gather.7.cloned.1.call-update) | async-done | bytes 16777232 | tf_op jit(solution)/shard_map/all_gather | solution.py:15
  353.3 65.8 %while.10 = (s32[]{:T(128)}, f32[2,64,512]{2,1,0:T(8,128)S(1)}, s32[]{:T(128)}, f32[64,2,64,512]{3,2,1,0:T(8,128)}, s32[]{:T(128)}, /*index=5*/s32[]{:T(128)}, s32[]{:T(128)}) while((s32[]{:T(128)}, f32[2,64,512]{2,1,0:T(8,128)S(1)}, s32[]{:T(128)}, f32[64,2,64,512]{3,2,1,0:T(8,128)}, s32[]{:T(128)}, /*index=5*/s32[]{:T(128)}, s32[]{:T(128)}) %tuple.30), condition=%wide.region_2.3_spmd, body=%wide.region_1.0_spmd.sunk | while | flops 65541 | bytes 786555 | solution.py:21
  353.4 1.0 bitcast_add_fusion.2
  354.4 1.0 bitcast_add_fusion.2
  355.5 1.0 bitcast_add_fusion.2
  356.5 1.0 bitcast_add_fusion.2
  357.5 1.0 bitcast_add_fusion.2
  358.6 1.0 bitcast_add_fusion.2
  359.6 1.0 bitcast_add_fusion.2
  360.7 1.0 bitcast_add_fusion.2
  361.7 1.0 bitcast_add_fusion.2
  362.8 1.0 bitcast_add_fusion.2
  363.8 1.0 bitcast_add_fusion.2
  364.9 1.0 bitcast_add_fusion.2
  365.9 1.0 bitcast_add_fusion.2
  366.9 1.0 bitcast_add_fusion.2
  368.0 1.0 bitcast_add_fusion.2
  369.0 1.0 bitcast_add_fusion.2
  370.1 1.0 bitcast_add_fusion.2
  371.1 1.0 bitcast_add_fusion.2
  372.2 1.0 bitcast_add_fusion.2
  373.2 1.0 bitcast_add_fusion.2
  374.3 1.0 bitcast_add_fusion.2
  375.3 1.0 bitcast_add_fusion.2
  376.3 1.0 bitcast_add_fusion.2
  377.4 1.0 bitcast_add_fusion.2
  378.4 1.0 bitcast_add_fusion.2
  379.5 1.0 bitcast_add_fusion.2
  380.5 1.0 bitcast_add_fusion.2
  381.6 1.0 bitcast_add_fusion.2
  382.6 1.0 bitcast_add_fusion.2
  383.6 1.0 bitcast_add_fusion.2
  384.7 1.0 bitcast_add_fusion.2
  385.7 1.0 bitcast_add_fusion.2
  386.8 1.0 bitcast_add_fusion.2
  387.8 1.0 bitcast_add_fusion.2
  388.9 1.0 bitcast_add_fusion.2
  389.9 1.0 bitcast_add_fusion.2
  391.0 1.0 bitcast_add_fusion.2
  392.0 1.0 bitcast_add_fusion.2
  393.0 1.0 bitcast_add_fusion.2
  394.1 1.0 bitcast_add_fusion.2
  395.1 1.0 bitcast_add_fusion.2
  396.2 1.0 bitcast_add_fusion.2
  397.2 1.0 bitcast_add_fusion.2
  398.3 1.0 bitcast_add_fusion.2
  399.3 1.0 bitcast_add_fusion.2
  400.4 1.0 bitcast_add_fusion.2
  401.4 1.0 bitcast_add_fusion.2
  402.4 1.0 bitcast_add_fusion.2
  403.5 1.0 bitcast_add_fusion.2
  404.5 1.0 bitcast_add_fusion.2
  405.6 1.0 bitcast_add_fusion.2
  406.6 1.0 bitcast_add_fusion.2
  407.7 1.0 bitcast_add_fusion.2
  417.1 1.0 bitcast_add_fusion.2
  (18 shorter events, 11.1 us)
Async XLA Ops:
  7.2 3.0 copy-start
  7.2 145.9 %all-gather.5.cloned.1.call-start = ((), (), s32[]{:S(2)}) async-start(), calls=%async_computation | async-start | bytes 18874368 | tf_op jit(solution)/shard_map/all_gather | solution.py:40
  7.2 48.0 %collective-permute-start = (bf16[1,512,2048]{2,1,0:T(8,128)(2,1)}, bf16[1,512,2048]{2,1,0:T(8,128)(2,1)S(1)}, u32[]{:S(2)}, u32[]{:S(2)}) collective-permute-start(bf16[1,512,2048]{2,1,0:T(8,128)(2,1)} %param.5), channel_id=1, source_target_pairs={{8,0},{16,8},{24,16},{32,24},{40,32},{48,40},{56,48},{64,56},{72,6... | collective-permute-start | bytes 6291464 | tf_op jit(solution)/shard_map/ppermute | solution.py:10
  58.0 295.3 %all-gather.7.cloned.1.call-start = ((), (), s32[]{:S(2)}) async-start(), calls=%async_computation.1 | async-start | bytes 17039360 | tf_op jit(solution)/shard_map/all_gather | solution.py:15
Sparse Core Ops, SparseCore 0:
  58.2 94.8 all-gather.4
  164.3 188.9 all-gather.6
